TPU v7x, 256 devices: a whole 4x4x8 slice. The times are simulated.
256 devices in a mesh: row: 16 (over z, core), col: 16 (over y, x).
Axes of the slice: x: 4, y: 4, z: 8, core: 2. Of those that a mesh axis runs over, the one named last changes fastest.
Arguments:
- inputs: bfloat16 [512, 16384], P('col', 'row'), may hold values from -6 to 6
- output_gradient: bfloat16 [512, 16384], P('col', 'row'), may hold values from -6 to 6
- gate_matrix: bfloat16 [16384, 26624], P('row', 'col'), may hold values from -0.046875 to 0.046875
- up_matrix: bfloat16 [16384, 26624], P('row', 'col'), may hold values from -0.046875 to 0.046875
- down_matrix: bfloat16 [26624, 16384], P('col', 'row'), may hold values from -0.046875 to 0.046875
- gate_adapter_first: bfloat16 [16384, 512], P('row', 'col'), may hold values from -0.046875 to 0.046875
- gate_adapter_second: bfloat16 [512, 26624], P('row', 'col'), may hold values from -0.25 to 0.25
- up_adapter_first: bfloat16 [16384, 512], P('row', 'col'), may hold values from -0.046875 to 0.046875
- up_adapter_second: bfloat16 [512, 26624], P('row', 'col'), may hold values from -0.25 to 0.25
- down_adapter_first: bfloat16 [26624, 512], P('col', 'row'), may hold values from -0.25 to 0.25
- down_adapter_second: bfloat16 [512, 16384], P('col', 'row'), may hold values from -0.046875 to 0.046875
Outputs:
- input_grad: bfloat16 [512, 16384], P('col', 'row')
- grad_gate_in: float32 [16384, 512], P('row', 'col')
- grad_gate_out: float32 [512, 26624], P('row', 'col')
- grad_up_in: float32 [16384, 512], P('row', 'col')
- grad_up_out: float32 [512, 26624], P('row', 'col')
- grad_down_in: float32 [26624, 512], P('col', 'row')
- grad_down_out: float32 [512, 16384], P('col', 'row')
All inputs are finite; a program needn't handle non-finite values.
Results may differ from a plain program's by a relative error of at most 0.0062.
Values may be sent and summed in bfloat16 or wider, within the bound.
No kernel may reach another device: no remote copies, remote signals or barrier semaphores. Data moves between devices by JAX's collectives and lax.ppermute only.
A program may use at most 128 MiB of HBM per device.

v0:
```python
import jax
import jax.numpy as jnp
from jax import lax
from jax.sharding import PartitionSpec as P


def matrix_product(first_mat, second_mat):
    return jnp.dot(first_mat, second_mat, preferred_element_type=jnp.float32)


def product_transposed(first_mat, second_mat):
    return lax.dot_general(
        first_mat, second_mat, (((1,), (1,)), ((), ())), preferred_element_type=jnp.float32
    )


def product_tn(first_mat, second_mat):
    return lax.dot_general(
        first_mat, second_mat, (((0,), (0,)), ((), ())), preferred_element_type=jnp.float32
    )


def gated_back(gate_pre, up_pre, hid_grad):
    sigmoid_g = jax.nn.sigmoid(gate_pre)
    silu_g = gate_pre * sigmoid_g
    hidden_state = (silu_g * up_pre).astype(jnp.bfloat16)
    gate_gradient = (hid_grad * up_pre * sigmoid_g * (1.0 + gate_pre * (1.0 - sigmoid_g))).astype(
        jnp.bfloat16
    )
    up_gradient = (hid_grad * silu_g).astype(jnp.bfloat16)
    return (hidden_state, gate_gradient, up_gradient)


def on_device(
    inputs,
    output_gradient,
    gate_matrix,
    up_matrix,
    down_matrix,
    gate_adapter_first,
    gate_adapter_second,
    up_adapter_first,
    up_adapter_second,
    down_adapter_first,
    down_adapter_second,
):
    row_index = lax.axis_index("row")
    col_index = lax.axis_index("col")
    input_row_block, cotangent_rows = (
        lax.all_gather(inputs, "col", axis=0, tiled=True),
        lax.all_gather(output_gradient, "col", axis=0, tiled=True),
    )
    rank_column = gate_adapter_first.shape[1]
    rank_row_index = gate_adapter_second.shape[0]
    portion_gate = matrix_product(input_row_block, gate_adapter_first)
    portion_up = matrix_product(input_row_block, up_adapter_first)
    portion_down = product_transposed(cotangent_rows, down_adapter_second)
    sum_gate, sum_up, sum_down = lax.psum((portion_gate, portion_up, portion_down), "row")
    reduced_gate, reduced_up, reduced_cotangent = (
        lax.all_gather(sum_gate.astype(jnp.bfloat16), "col", axis=1, tiled=True),
        lax.all_gather(sum_up.astype(jnp.bfloat16), "col", axis=1, tiled=True),
        lax.all_gather(sum_down.astype(jnp.bfloat16), "col", axis=1, tiled=True),
    )
    row_start = row_index * rank_row_index
    reduced_gate_row = lax.dynamic_slice_in_dim(reduced_gate, row_start, rank_row_index, 1)
    reduced_up_row = lax.dynamic_slice_in_dim(reduced_up, row_start, rank_row_index, 1)
    reduced_cotangent_row = lax.dynamic_slice_in_dim(
        reduced_cotangent, row_start, rank_row_index, 1
    )
    gate_portion = matrix_product(input_row_block, gate_matrix) + matrix_product(
        reduced_gate_row, gate_adapter_second
    )
    up_portion = matrix_product(input_row_block, up_matrix) + matrix_product(
        reduced_up_row, up_adapter_second
    )
    hidden_portion = product_transposed(cotangent_rows, down_matrix) + product_transposed(
        reduced_cotangent_row, down_adapter_first
    )
    gate_pre, up_pre, hid_grad = (
        lax.psum_scatter(gate_portion, "row", scatter_dimension=0, tiled=True),
        lax.psum_scatter(up_portion, "row", scatter_dimension=0, tiled=True),
        lax.psum_scatter(hidden_portion, "row", scatter_dimension=0, tiled=True),
    )
    hidden_state, gate_gradient, up_gradient = gated_back(gate_pre, up_pre, hid_grad)
    hidden_complete, gate_complete, up_complete = (
        lax.all_gather(hidden_state, "row", axis=0, tiled=True),
        lax.all_gather(gate_gradient, "row", axis=0, tiled=True),
        lax.all_gather(up_gradient, "row", axis=0, tiled=True),
    )
    gate_cotangent = product_transposed(gate_complete, gate_adapter_second)
    up_cotangent = product_transposed(up_complete, up_adapter_second)
    hidden_cotangent = matrix_product(hidden_complete, down_adapter_first)
    sum_bgate, sum_bup, sum_bhidden = lax.psum(
        (gate_cotangent, up_cotangent, hidden_cotangent), "col"
    )
    gate_low, up_low, hidden_reduced = (
        lax.all_gather(sum_bgate.astype(jnp.bfloat16), "row", axis=1, tiled=True),
        lax.all_gather(sum_bup.astype(jnp.bfloat16), "row", axis=1, tiled=True),
        lax.all_gather(sum_bhidden.astype(jnp.bfloat16), "row", axis=1, tiled=True),
    )
    col_start = col_index * rank_column
    gate_reduced_column = lax.dynamic_slice_in_dim(gate_low, col_start, rank_column, 1)
    up_reduced_column = lax.dynamic_slice_in_dim(up_low, col_start, rank_column, 1)
    hidden_low_col = lax.dynamic_slice_in_dim(hidden_reduced, col_start, rank_column, 1)
    input_portion = product_transposed(gate_complete, gate_matrix) + product_transposed(
        up_complete, up_matrix
    )
    input_portion = (
        input_portion
        + product_transposed(gate_reduced_column, gate_adapter_first)
        + product_transposed(up_reduced_column, up_adapter_first)
    )
    input_grad = lax.psum_scatter(input_portion, "col", scatter_dimension=0, tiled=True).astype(
        jnp.bfloat16
    )
    grad_gate_in = product_tn(input_row_block, gate_reduced_column)
    grad_gate_out = product_tn(reduced_gate_row, gate_complete)
    grad_up_in = product_tn(input_row_block, up_reduced_column)
    grad_up_out = product_tn(reduced_up_row, up_complete)
    grad_down_in = product_tn(hidden_complete, reduced_cotangent_row)
    grad_down_out = product_tn(hidden_low_col, cotangent_rows)
    return (
        input_grad,
        grad_gate_in,
        grad_gate_out,
        grad_up_in,
        grad_up_out,
        grad_down_in,
        grad_down_out,
    )


def solution(mesh):
    return jax.shard_map(
        on_device,
        mesh=mesh,
        in_specs=(
            P("col", "row"),
            P("col", "row"),
            P("row", "col"),
            P("row", "col"),
            P("col", "row"),
            P("row", "col"),
            P("row", "col"),
            P("row", "col"),
            P("row", "col"),
            P("col", "row"),
            P("col", "row"),
        ),
        out_specs=(
            P("col", "row"),
            P("row", "col"),
            P("row", "col"),
            P("row", "col"),
            P("row", "col"),
            P("col", "row"),
            P("col", "row"),
        ),
        check_vma=False,
    )
```

profile of v0, /device:TPU:2, one launch (start us, length us, event | category | flops | bytes accessed | tf_op | source)
XLA Modules:
  0.0 705.9 jit_solution(5695515283411741139)
XLA Ops:
  8.7 51.8 %all-gather.6.cloned.1.call-done = bf16[512,1024]{1,0:T(8,128)(2,1)} async-done(((bf16[32,1024]{1,0:T(8,128)(2,1)}), bf16[512,1024]{1,0:T(8,128)(2,1)}) %all-gather.6.cloned.1.call-update) | async-done | bytes 1048592 | tf_op jit(solution)/shard_map/all_gather | solution.py:51
  62.2 47.7 %all-gather.8.cloned.1.call-done = bf16[512,1024]{1,0:T(8,128)(2,1)} async-done(((bf16[32,1024]{1,0:T(8,128)(2,1)}), bf16[512,1024]{1,0:T(8,128)(2,1)}) %all-gather.8.cloned.1.call-update) | async-done | bytes 1048592 | tf_op jit(solution)/shard_map/all_gather | solution.py:50
  109.9 2.3 fusion.33
  112.2 2.3 fusion.31
  114.5 48.4 %all-reduce.4 = (bf16[512,32]{0,1:T(8,128)(2,1)}, bf16[512,32]{0,1:T(8,128)(2,1)S(1)}, bf16[512,32]{0,1:T(8,128)(2,1)}) all-reduce(f32[512,32]{0,1:T(8,128)} %fusion.33, f32[512,32]{0,1:T(8,128)S(1)} %fusion.29, f32[512,32]{0,1:T(8,128)} %fusion.31), channel_id=1, replica_groups=mesh['row'=16,'col'=16] {'row'}, use_global_device_ids=true, to_apply=%region_4.0 | all-reduce | flops 49152 | bytes 294912 | tf_op jit(solution)/shard_map/psum | solution.py:58
  162.8 22.4 %all_gather.34 = bf16[512,512]{0,1:T(8,128)(2,1)S(1)} all-gather(bf16[512,32]{0,1:T(8,128)(2,1)S(1)} %get-tuple-element.11), channel_id=1, replica_groups=mesh['row'=16,'col'=16] {'col'}, dimensions={1}, use_global_device_ids=true | all-gather | bytes 557056 | tf_op jit(solution)/shard_map/all_gather | solution.py:62
  185.3 4.6 fusion.28
  189.9 2.3 convolution_add_fusion.2
  193.0 22.6 %all_gather.37 = bf16[512,512]{0,1:T(8,128)(2,1)S(1)} all-gather(bf16[512,32]{0,1:T(8,128)(2,1)S(1)} %copy-done.21), channel_id=1, replica_groups=mesh['row'=16,'col'=16] {'col'}, dimensions={1}, use_global_device_ids=true | all-gather | bytes 557056 | tf_op jit(solution)/shard_map/all_gather | solution.py:60
  215.6 3.5 fusion.32
  219.1 2.4 convolution_add_fusion
  222.3 22.4 %all_gather.36 = bf16[512,512]{0,1:T(8,128)(2,1)S(1)} all-gather(bf16[512,32]{0,1:T(8,128)(2,1)S(1)} %copy-done.19), channel_id=1, replica_groups=mesh['row'=16,'col'=16] {'col'}, dimensions={1}, use_global_device_ids=true | all-gather | bytes 557056 | tf_op jit(solution)/shard_map/all_gather | solution.py:61
  244.7 4.6 fusion.30
  249.3 2.4 convolution_add_fusion.1
  251.8 2.9 reduce-scatter.5.cloned.1.call-done
  254.7 62.9 %reduce-scatter.9.cloned.1.call-done = f32[32,1664]{1,0:T(8,128)} async-done(((f32[512,1664]{1,0:T(8,128)}), f32[32,1664]{1,0:T(8,128)}) %reduce-scatter.9.cloned.1.call-update) | async-done | bytes 213008 | tf_op jit(solution)/shard_map/reduce_scatter | solution.py:80
  317.6 63.1 %reduce-scatter.7.cloned.1.call-done = f32[32,1664]{1,0:T(8,128)} async-done(((f32[512,1664]{1,0:T(8,128)}), f32[32,1664]{1,0:T(8,128)}) %reduce-scatter.7.cloned.1.call-update) | async-done | bytes 213008 | tf_op jit(solution)/shard_map/reduce_scatter | solution.py:81
  384.2 36.6 %all-gather.14.cloned.1.call-done = bf16[512,1664]{1,0:T(8,128)(2,1)} async-done(((bf16[32,1664]{1,0:T(8,128)(2,1)}), bf16[512,1664]{1,0:T(8,128)(2,1)}) %all-gather.14.cloned.1.call-update) | async-done | bytes 1703952 | tf_op jit(solution)/shard_map/all_gather | solution.py:86
  420.8 2.7 fusion.38
  423.5 37.5 %all-gather.12.cloned.1.call-done = bf16[512,1664]{1,0:T(8,128)(2,1)} async-done(((bf16[32,1664]{1,0:T(8,128)(2,1)}), bf16[512,1664]{1,0:T(8,128)(2,1)}) %all-gather.12.cloned.1.call-update) | async-done | bytes 1703952 | tf_op jit(solution)/shard_map/all_gather | solution.py:88
  461.0 2.7 fusion.37
  463.7 37.5 %all-gather.10.cloned.1.call-done = bf16[512,1664]{1,0:T(8,128)(2,1)} async-done(((bf16[32,1664]{1,0:T(8,128)(2,1)}), bf16[512,1664]{1,0:T(8,128)(2,1)}) %all-gather.10.cloned.1.call-update) | async-done | bytes 1703952 | tf_op jit(solution)/shard_map/all_gather | solution.py:87
  501.2 2.7 fusion.36
  503.9 72.1 %all-reduce.5 = (bf16[512,32]{0,1:T(8,128)(2,1)}, bf16[512,32]{0,1:T(8,128)(2,1)}, bf16[512,32]{0,1:T(8,128)(2,1)}) all-reduce(f32[512,32]{0,1:T(8,128)} %fusion.36, f32[512,32]{0,1:T(8,128)} %fusion.37, f32[512,32]{0,1:T(8,128)S(1)} %copy-done.18), channel_id=1, replica_groups=mesh['row'=16,'col'=16] {'col'}, use_global_device_ids=true, to_apply=%region_6.0 | all-reduce | flops 49152 | bytes 294912 | tf_op jit(solution)/shard_map/psum | solution.py:93
  576.1 17.3 %all_gather.40 = bf16[512,512]{0,1:T(8,128)(2,1)S(1)} all-gather(bf16[512,32]{0,1:T(8,128)(2,1)} %get-tuple-element.7), channel_id=1, replica_groups=mesh['row'=16,'col'=16] {'row'}, dimensions={1}, use_global_device_ids=true | all-gather | bytes 557056 | tf_op jit(solution)/shard_map/all_gather | solution.py:97
  593.4 16.5 %all_gather.41 = bf16[512,512]{0,1:T(8,128)(2,1)S(1)} all-gather(bf16[512,32]{0,1:T(8,128)(2,1)} %get-tuple-element.8), channel_id=1, replica_groups=mesh['row'=16,'col'=16] {'row'}, dimensions={1}, use_global_device_ids=true | all-gather | bytes 557056 | tf_op jit(solution)/shard_map/all_gather | solution.py:98
  610.5 2.1 fusion.34
  612.9 2.1 fusion.35
  617.6 17.8 %all_gather.43 = bf16[512,512]{0,1:T(8,128)(2,1)S(1)} all-gather(bf16[512,32]{0,1:T(8,128)(2,1)S(1)} %copy-done.20), channel_id=1, replica_groups=mesh['row'=16,'col'=16] {'row'}, dimensions={1}, use_global_device_ids=true | all-gather | bytes 557056 | tf_op jit(solution)/shard_map/all_gather | solution.py:99
  635.4 2.2 convolution_bitcast_fusion.1
  637.6 2.3 convolution_bitcast_fusion
  646.6 51.2 %reduce-scatter.11.cloned.1.call-done = f32[32,1024]{1,0:T(8,128)} async-done(((f32[512,1024]{1,0:T(8,128)}), f32[32,1024]{1,0:T(8,128)}) %reduce-scatter.11.cloned.1.call-update) | async-done | bytes 131088 | tf_op jit(solution)/shard_map/reduce_scatter | solution.py:113
  (73 shorter events, 19.8 us)
Async XLA Ops:
  7.2 208.4 %copy-start = (bf16[1024,1664]{1,0:T(8,128)(2,1)S(1)}, bf16[1024,1664]{1,0:T(8,128)(2,1)}, u32[]{:S(2)}) copy-start(bf16[1024,1664]{1,0:T(8,128)(2,1)} %param.13) | copy-start | bytes 10223620
  7.2 105.0 %copy-start.15 = (bf16[1024,32]{0,1:T(8,128)(2,1)S(1)}, bf16[1024,32]{0,1:T(8,128)(2,1)}, u32[]{:S(2)}) copy-start(bf16[1024,32]{0,1:T(8,128)(2,1)} %param.18) | copy-start | bytes 196612
  7.2 53.4 %all-gather.6.cloned.1.call-start = ((), (), s32[]{:S(2)}) async-start(), calls=%async_computation.4 | async-start | bytes 1114112 | tf_op jit(solution)/shard_map/all_gather | solution.py:51
  7.9 102.0 %all-gather.8.cloned.1.call-start = ((), (), s32[]{:S(2)}) async-start(), calls=%async_computation.6 | async-start | bytes 1114112 | tf_op jit(solution)/shard_map/all_gather | solution.py:50
  8.7 246.0 %reduce-scatter.5.cloned.1.call-start = ((), (), s32[]{:S(2)}) async-start(), calls=%async_computation.5 | async-start | bytes 3620864 | tf_op jit(solution)/shard_map/reduce_scatter | solution.py:82
  185.3 4.6 copy-start.7
  185.3 4.6 copy-start.12
  192.2 0.8 copy-start.21
  192.3 125.3 %reduce-scatter.9.cloned.1.call-start = ((), (), s32[]{:S(2)}) async-start(), calls=%async_computation.8 | async-start | bytes 3620864 | tf_op jit(solution)/shard_map/reduce_scatter | solution.py:80
  215.6 3.5 copy-start.8
  215.6 3.5 copy-start.14
  221.5 0.8 copy-start.19
  221.5 159.1 %reduce-scatter.7.cloned.1.call-start = ((), (), s32[]{:S(2)}) async-start(), calls=%async_computation.7 | async-start | bytes 3620864 | tf_op jit(solution)/shard_map/reduce_scatter | solution.py:81
  244.7 4.6 copy-start.9
  244.7 4.6 copy-start.13
  251.8 169.0 %all-gather.14.cloned.1.call-start = ((), (), s32[]{:S(2)}) async-start(), calls=%async_computation.12 | async-start | bytes 1810432 | tf_op jit(solution)/shard_map/all_gather | solution.py:86
  382.7 78.4 %all-gather.12.cloned.1.call-start = ((), (), s32[]{:S(2)}) async-start(), calls=%async_computation.10 | async-start | bytes 1810432 | tf_op jit(solution)/shard_map/all_gather | solution.py:88
  383.4 117.8 %all-gather.10.cloned.1.call-start = ((), (), s32[]{:S(2)}) async-start(), calls=%async_computation.9 | async-start | bytes 1810432 | tf_op jit(solution)/shard_map/all_gather | solution.py:87
  384.2 313.7 %reduce-scatter.11.cloned.1.call-start = ((), (), s32[]{:S(2)}) async-start(), calls=%async_computation.11 | async-start | bytes 2228224 | tf_op jit(solution)/shard_map/reduce_scatter | solution.py:113
  423.5 80.4 %copy-start.18 = (f32[512,32]{0,1:T(8,128)S(1)}, f32[512,32]{0,1:T(8,128)}, u32[]{:S(2)}) copy-start(f32[512,32]{0,1:T(8,128)} %fusion.38) | copy-start | bytes 196612
  423.5 186.5 %copy-start.17 = (bf16[1024,32]{0,1:T(8,128)(2,1)S(1)}, bf16[1024,32]{0,1:T(8,128)(2,1)}, u32[]{:S(2)}) copy-start(bf16[1024,32]{0,1:T(8,128)(2,1)} %param.16) | copy-start | bytes 196612
  576.1 34.3 %copy-start.4 = (bf16[512,1664]{1,0:T(8,128)(2,1)S(1)}, bf16[512,1664]{1,0:T(8,128)(2,1)}, u32[]{:S(2)}) copy-start(bf16[512,1664]{1,0:T(8,128)(2,1)} %all-gather.10.cloned.1.call-done) | copy-start | bytes 5111812
  593.4 16.5 %copy-start.11 = (bf16[512,512]{0,1:T(8,128)(2,1)}, bf16[512,512]{0,1:T(8,128)(2,1)S(1)}, u32[]{:S(2)}) copy-start(bf16[512,512]{0,1:T(8,128)(2,1)S(1)} %all_gather.40) | copy-start | bytes 1572868
  610.0 5.0 copy-start.10
  610.4 2.1 copy-start.2
  610.4 2.5 copy-start.22
  612.9 2.1 copy-start.16
  616.8 0.8 copy-start.20
  616.9 23.1 %copy-start.6 = (bf16[512,1024]{1,0:T(8,128)(2,1)S(1)}, bf16[512,1024]{1,0:T(8,128)(2,1)}, u32[]{:S(2)}) copy-start(bf16[512,1024]{1,0:T(8,128)(2,1)} %all-gather.6.cloned.1.call-done) | copy-start | bytes 3145732
  617.6 23.3 %copy-start.1 = (bf16[512,1664]{1,0:T(8,128)(2,1)S(1)}, bf16[512,1664]{1,0:T(8,128)(2,1)}, u32[]{:S(2)}) copy-start(bf16[512,1664]{1,0:T(8,128)(2,1)} %all-gather.14.cloned.1.call-done) | copy-start | bytes 5111812
  637.6 5.3 copy-start.5
  640.9 3.8 copy-start.3
Sparse Core Ops, SparseCore 0:
  10.4 50.0 all-gather.5
  63.0 46.8 all-gather.7
  192.4 62.2 reduce-scatter.4
  257.1 60.4 reduce-scatter.8
  320.0 60.6 reduce-scatter.6
  382.9 37.8 all-gather.13
  423.2 37.7 all-gather.11
  463.4 37.7 all-gather.9
  617.0 80.7 reduce-scatter.10
where the time goes:
time: 707 us; the launch traced here: 706 us
  waiting for transfers between devices  394 us (56%)
  blocking collectives  240 us (34%)
  matrix products  51.7 us (7%)
  between operations  14.1 us (2%)
    psum x1, blocking collectives, on_device(): lax.psum((gate_cotangent, up_cotangent, hidden_cotangent), 'col')  72.1 us
    reduce_scatter x1, waiting for transfers between devices, on_device(): lax.psum_scatter(up_portion, 'row', scatter_dimension=0, tiled=True)  63.1 us
    reduce_scatter x1, waiting for transfers between devices, on_device(): lax.psum_scatter(gate_portion, 'row', scatter_dimension=0, tiled=True)  62.9 us
    all_gather x1, waiting for transfers between devices, on_device(): lax.all_gather(output_gradient, 'col', axis=0, tiled=True)  51.8 us
    reduce_scatter x1, waiting for transfers between devices, on_device(): lax.psum_scatter(input_portion, 'col', scatter_dimension=0, tiled=True)  51.2 us
    psum x1, blocking collectives, on_device(): lax.psum((portion_gate, portion_up, portion_down), 'row')  48.4 us
    all_gather x1, waiting for transfers between devices, on_device(): lax.all_gather(inputs, 'col', axis=0, tiled=True)  47.7 us
    all_gather x1, waiting for transfers between devices, on_device(): lax.all_gather(gate_gradient, 'row', axis=0, tiled=True)  37.5 us
  transfers between devices with their start and end apart: 9, of which 9 were waited for; matrix products, arithmetic and copies ran while one was open for 4% of the time, Pallas kernels for 0%

commit v1 on v0

--- a/solution.py
+++ b/solution.py
@@ -2,6 +2,12 @@
 import jax.numpy as jnp
 from jax import lax
 from jax.sharding import PartitionSpec as P
+
+
+def solve_tiles_now(arr_in, peer_axis):
+    y2 = jnp.stack([arr_in for _ in range(lax.axis_size(peer_axis))])
+    field_out = lax.all_to_all(y2, axis_name=peer_axis, split_axis=0, concat_axis=0)
+    return jnp.concatenate(field_out, axis=0)
 
 
 def matrix_product(first_mat, second_mat):
@@ -85,7 +91,7 @@
     hidden_complete, gate_complete, up_complete = (
         lax.all_gather(hidden_state, "row", axis=0, tiled=True),
         lax.all_gather(gate_gradient, "row", axis=0, tiled=True),
-        lax.all_gather(up_gradient, "row", axis=0, tiled=True),
+        solve_tiles_now(up_gradient, "row"),
     )
     gate_cotangent = product_transposed(gate_complete, gate_adapter_second)
     up_cotangent = product_transposed(up_complete, up_adapter_second)

time: 707 us -> 685 us (0.969)
  waiting for transfers between devices: 394 us -> 362 us
    all_gather x1 -> x0, waiting for transfers between devices: 37.5 us -> none  [on_device(): lax.all_gather(up_gradient, 'row', axis=0, tiled=True)]
    all_gather x1, waiting for transfers between devices: 36.6 us -> 46.4 us  [on_device(): lax.all_gather(hidden_state, 'row', axis=0, tiled=True)]
  transfers between devices with their start and end apart: 9 -> 9, of which waited for: 9 -> 8; matrix products, arithmetic and copies ran while one was open for 4% -> 6% of each run, Pallas kernels for 0% -> 0%
where the time goes in v1:
time: 685 us; the launch traced here: 684 us
  waiting for transfers between devices  362 us (53%)
  blocking collectives  239 us (35%)
  matrix products  58.3 us (9%)
  between operations  14.4 us (2%)
    psum x1, blocking collectives, on_device(): lax.psum((gate_cotangent, up_cotangent, hidden_cotangent), 'col')  71.6 us
    reduce_scatter x1, waiting for transfers between devices, on_device(): lax.psum_scatter(up_portion, 'row', scatter_dimension=0, tiled=True)  63.1 us
    reduce_scatter x1, waiting for transfers between devices, on_device(): lax.psum_scatter(gate_portion, 'row', scatter_dimension=0, tiled=True)  63 us
    all_gather x1, waiting for transfers between devices, on_device(): lax.all_gather(output_gradient, 'col', axis=0, tiled=True)  51.8 us
    reduce_scatter x1, waiting for transfers between devices, on_device(): lax.psum_scatter(input_portion, 'col', scatter_dimension=0, tiled=True)  51.2 us
    psum x1, blocking collectives, on_device(): lax.psum((portion_gate, portion_up, portion_down), 'row')  48.9 us
    all_gather x1, waiting for transfers between devices, on_device(): lax.all_gather(inputs, 'col', axis=0, tiled=True)  47.7 us
    all_gather x1, waiting for transfers between devices, on_device(): lax.all_gather(hidden_state, 'row', axis=0, tiled=True)  46.4 us
  transfers between devices with their start and end apart: 9, of which 8 were waited for; matrix products, arithmetic and copies ran while one was open for 6% of the time, Pallas kernels for 0%

profile of v1, /device:TPU:2, one launch (start us, length us, event | category | flops | bytes accessed | tf_op | source)
XLA Modules:
  0.0 683.5 jit_solution(13827126708538852089)
XLA Ops:
  8.7 51.8 %all-gather.5.cloned.1.call-done = bf16[512,1024]{1,0:T(8,128)(2,1)} async-done(((bf16[32,1024]{1,0:T(8,128)(2,1)}), bf16[512,1024]{1,0:T(8,128)(2,1)}) %all-gather.5.cloned.1.call-update) | async-done | bytes 1048592 | tf_op jit(solution)/shard_map/all_gather | solution.py:57
  62.2 47.7 %all-gather.7.cloned.1.call-done = bf16[512,1024]{1,0:T(8,128)(2,1)} async-done(((bf16[32,1024]{1,0:T(8,128)(2,1)}), bf16[512,1024]{1,0:T(8,128)(2,1)}) %all-gather.7.cloned.1.call-update) | async-done | bytes 1048592 | tf_op jit(solution)/shard_map/all_gather | solution.py:56
  109.9 2.3 fusion.33
  112.2 2.3 fusion.31
  114.5 48.9 %all-reduce.4 = (bf16[512,32]{0,1:T(8,128)(2,1)S(1)}, bf16[512,32]{0,1:T(8,128)(2,1)}, bf16[512,32]{0,1:T(8,128)(2,1)S(1)}) all-reduce(f32[512,32]{0,1:T(8,128)} %fusion.33, f32[512,32]{0,1:T(8,128)S(1)} %fusion.29, f32[512,32]{0,1:T(8,128)} %fusion.31), channel_id=1, replica_groups=mesh['row'=16,'col'=16] {'row'}, use_global_device_ids=true, to_apply=%region_4.0 | all-reduce | flops 49152 | bytes 294912 | tf_op jit(solution)/shard_map/psum | solution.py:64
  163.4 22.5 %all_gather.31 = bf16[512,512]{0,1:T(8,128)(2,1)S(1)} all-gather(bf16[512,32]{0,1:T(8,128)(2,1)} %get-tuple-element.11), channel_id=1, replica_groups=mesh['row'=16,'col'=16] {'col'}, dimensions={1}, use_global_device_ids=true | all-gather | bytes 557056 | tf_op jit(solution)/shard_map/all_gather | solution.py:68
  185.9 4.6 fusion.28
  190.5 2.4 convolution_add_fusion.2
  193.0 22.6 %all_gather.34 = bf16[512,512]{0,1:T(8,128)(2,1)S(1)} all-gather(bf16[512,32]{0,1:T(8,128)(2,1)S(1)} %get-tuple-element.10), channel_id=1, replica_groups=mesh['row'=16,'col'=16] {'col'}, dimensions={1}, use_global_device_ids=true | all-gather | bytes 557056 | tf_op jit(solution)/shard_map/all_gather | solution.py:66
  215.6 4.6 fusion.32
  220.2 2.4 convolution_add_fusion
  222.6 22.4 %all_gather.33 = bf16[512,512]{0,1:T(8,128)(2,1)S(1)} all-gather(bf16[512,32]{0,1:T(8,128)(2,1)S(1)} %get-tuple-element.12), channel_id=1, replica_groups=mesh['row'=16,'col'=16] {'col'}, dimensions={1}, use_global_device_ids=true | all-gather | bytes 557056 | tf_op jit(solution)/shard_map/all_gather | solution.py:67
  245.1 3.5 fusion.30
  248.6 2.4 convolution_add_fusion.1
  251.1 2.9 reduce-scatter.5.cloned.1.call-done
  254.1 63.0 %reduce-scatter.9.cloned.1.call-done = f32[32,1664]{1,0:T(8,128)} async-done(((f32[512,1664]{1,0:T(8,128)}), f32[32,1664]{1,0:T(8,128)}) %reduce-scatter.9.cloned.1.call-update) | async-done | bytes 213008 | tf_op jit(solution)/shard_map/reduce_scatter | solution.py:86
  317.1 63.1 %reduce-scatter.7.cloned.1.call-done = f32[32,1664]{1,0:T(8,128)} async-done(((f32[512,1664]{1,0:T(8,128)}), f32[32,1664]{1,0:T(8,128)}) %reduce-scatter.7.cloned.1.call-update) | async-done | bytes 213008 | tf_op jit(solution)/shard_map/reduce_scatter | solution.py:87
  383.4 4.7 all-to-all-start
  389.1 46.4 %all-gather.11.cloned.1.call-done = bf16[512,1664]{1,0:T(8,128)(2,1)} async-done(((bf16[32,1664]{1,0:T(8,128)(2,1)}), bf16[512,1664]{1,0:T(8,128)(2,1)}) %all-gather.11.cloned.1.call-update) | async-done | bytes 1703952 | tf_op jit(solution)/shard_map/all_gather | solution.py:92
  435.5 2.7 fusion.38
  438.2 2.7 fusion.37
  440.9 4.9 fusion.35
  445.8 33.4 %all-gather.9.cloned.1.call-done = bf16[512,1664]{1,0:T(8,128)(2,1)} async-done(((bf16[32,1664]{1,0:T(8,128)(2,1)}), bf16[512,1664]{1,0:T(8,128)(2,1)}) %all-gather.9.cloned.1.call-update) | async-done | bytes 1703952 | tf_op jit(solution)/shard_map/all_gather | solution.py:93
  479.2 2.7 fusion.36
  481.9 71.6 %all-reduce.5 = (bf16[512,32]{0,1:T(8,128)(2,1)S(1)}, bf16[512,32]{0,1:T(8,128)(2,1)S(1)}, bf16[512,32]{0,1:T(8,128)(2,1)S(1)}) all-reduce(f32[512,32]{0,1:T(8,128)} %fusion.36, f32[512,32]{0,1:T(8,128)} %fusion.37, f32[512,32]{0,1:T(8,128)} %fusion.38), channel_id=1, replica_groups=mesh['row'=16,'col'=16] {'col'}, use_global_device_ids=true, to_apply=%region_6.0 | all-reduce | flops 49152 | bytes 294912 | tf_op jit(solution)/shard_map/psum | solution.py:99
  553.5 17.1 %all_gather.36 = bf16[512,512]{0,1:T(8,128)(2,1)S(1)} all-gather(bf16[512,32]{0,1:T(8,128)(2,1)S(1)} %get-tuple-element.7), channel_id=1, replica_groups=mesh['row'=16,'col'=16] {'row'}, dimensions={1}, use_global_device_ids=true | all-gather | bytes 557056 | tf_op jit(solution)/shard_map/all_gather | solution.py:103
  570.6 16.1 %all_gather.37 = bf16[512,512]{0,1:T(8,128)(2,1)S(1)} all-gather(bf16[512,32]{0,1:T(8,128)(2,1)S(1)} %get-tuple-element.8), channel_id=1, replica_groups=mesh['row'=16,'col'=16] {'row'}, dimensions={1}, use_global_device_ids=true | all-gather | bytes 557056 | tf_op jit(solution)/shard_map/all_gather | solution.py:104
  588.1 4.2 fusion.34
  594.2 17.9 %all_gather.39 = bf16[512,512]{0,1:T(8,128)(2,1)S(1)} all-gather(bf16[512,32]{0,1:T(8,128)(2,1)S(1)} %get-tuple-element.9), channel_id=1, replica_groups=mesh['row'=16,'col'=16] {'row'}, dimensions={1}, use_global_device_ids=true | all-gather | bytes 557056 | tf_op jit(solution)/shard_map/all_gather | solution.py:105
  614.3 2.3 convolution_bitcast_fusion
  617.5 2.7 fusion.11
  624.0 51.2 %reduce-scatter.11.cloned.1.call-done = f32[32,1024]{1,0:T(8,128)} async-done(((f32[512,1024]{1,0:T(8,128)}), f32[32,1024]{1,0:T(8,128)}) %reduce-scatter.11.cloned.1.call-update) | async-done | bytes 131088 | tf_op jit(solution)/shard_map/reduce_scatter | solution.py:119
  (63 shorter events, 19.2 us)
Async XLA Ops:
  7.2 237.9 %copy-start = (bf16[1024,1664]{1,0:T(8,128)(2,1)S(1)}, bf16[1024,1664]{1,0:T(8,128)(2,1)}, u32[]{:S(2)}) copy-start(bf16[1024,1664]{1,0:T(8,128)(2,1)} %param.14) | copy-start | bytes 10223620
  7.2 105.0 %copy-start.16 = (bf16[1024,32]{0,1:T(8,128)(2,1)S(1)}, bf16[1024,32]{0,1:T(8,128)(2,1)}, u32[]{:S(2)}) copy-start(bf16[1024,32]{0,1:T(8,128)(2,1)} %param.18) | copy-start | bytes 196612
  7.2 53.4 %all-gather.5.cloned.1.call-start = ((), (), s32[]{:S(2)}) async-start(), calls=%async_computation.5 | async-start | bytes 1114112 | tf_op jit(solution)/shard_map/all_gather | solution.py:57
  7.9 102.0 %all-gather.7.cloned.1.call-start = ((), (), s32[]{:S(2)}) async-start(), calls=%async_computation.7 | async-start | bytes 1114112 | tf_op jit(solution)/shard_map/all_gather | solution.py:56
  8.7 245.4 %reduce-scatter.5.cloned.1.call-start = ((), (), s32[]{:S(2)}) async-start(), calls=%async_computation.6 | async-start | bytes 3620864 | tf_op jit(solution)/shard_map/reduce_scatter | solution.py:88
  185.9 4.6 copy-start.6
  185.9 4.6 copy-start.11
  192.9 124.1 %reduce-scatter.9.cloned.1.call-start = ((), (), s32[]{:S(2)}) async-start(), calls=%async_computation.9 | async-start | bytes 3620864 | tf_op jit(solution)/shard_map/reduce_scatter | solution.py:86
  215.5 4.6 copy-start.7
  215.5 4.6 copy-start.14
  222.6 157.5 %reduce-scatter.7.cloned.1.call-start = ((), (), s32[]{:S(2)}) async-start(), calls=%async_computation.8 | async-start | bytes 3620864 | tf_op jit(solution)/shard_map/reduce_scatter | solution.py:87
  245.1 3.5 copy-start.8
  245.1 3.5 copy-start.13
  251.1 184.4 %all-gather.11.cloned.1.call-start = ((), (), s32[]{:S(2)}) async-start(), calls=%async_computation.12 | async-start | bytes 1810432 | tf_op jit(solution)/shard_map/all_gather | solution.py:92
  383.4 52.1 %copy-start.12 = (bf16[1664,32]{0,1:T(8,128)(2,1)S(1)}, bf16[1664,32]{0,1:T(8,128)(2,1)}, u32[]{:S(2)}) copy-start(bf16[1664,32]{0,1:T(8,128)(2,1)} %param.20) | copy-start | bytes 319492
  383.4 54.8 %all-to-all-start = ((bf16[16,32,1664]{2,1,0:T(8,128)(2,1)}), bf16[16,32,1664]{2,1,0:T(8,128)(2,1)}, u32[]{:S(2)}, u32[]{:S(2)}) async-start(bf16[16,32,1664]{2,1,0:T(8,128)(2,1)} %stack.2), calls=%async_computation.3 | async-start | bytes 3407872 | tf_op jit(solution)/shard_map/all_to_all | solution.py:9
  388.1 91.1 %all-gather.9.cloned.1.call-start = ((), (), s32[]{:S(2)}) async-start(), calls=%async_computation.10 | async-start | bytes 1810432 | tf_op jit(solution)/shard_map/all_gather | solution.py:93
  388.9 286.2 %reduce-scatter.11.cloned.1.call-start = ((), (), s32[]{:S(2)}) async-start(), calls=%async_computation.11 | async-start | bytes 2228224 | tf_op jit(solution)/shard_map/reduce_scatter | solution.py:119
  440.9 38.3 %copy-start.15 = (bf16[32,1664]{1,0:T(8,128)(2,1)S(1)}, bf16[32,1664]{1,0:T(8,128)(2,1)}, u32[]{:S(2)}) copy-start(bf16[32,1664]{1,0:T(8,128)(2,1)} %param.17) | copy-start | bytes 319492
  553.5 34.6 %copy-start.2 = (bf16[512,1664]{1,0:T(8,128)(2,1)S(1)}, bf16[512,1664]{1,0:T(8,128)(2,1)}, u32[]{:S(2)}) copy-start(bf16[512,1664]{1,0:T(8,128)(2,1)} %all-gather.9.cloned.1.call-done) | copy-start | bytes 5111812
  570.6 16.1 %copy-start.10 = (bf16[512,512]{0,1:T(8,128)(2,1)}, bf16[512,512]{0,1:T(8,128)(2,1)S(1)}, u32[]{:S(2)}) copy-start(bf16[512,512]{0,1:T(8,128)(2,1)S(1)} %all_gather.36) | copy-start | bytes 1572868
  586.7 5.6 copy-start.9
  588.1 4.3 copy-start.5
  588.1 4.3 copy-start.17
  594.2 22.4 %copy-start.4 = (bf16[512,1024]{1,0:T(8,128)(2,1)S(1)}, bf16[512,1024]{1,0:T(8,128)(2,1)}, u32[]{:S(2)}) copy-start(bf16[512,1024]{1,0:T(8,128)(2,1)} %all-gather.5.cloned.1.call-done) | copy-start | bytes 3145732
  614.3 6.0 copy-start.1
  617.5 4.6 copy-start.3
Sparse Core Ops, SparseCore 0:
  10.4 50.0 all-gather.4
  63.0 46.8 all-gather.6
  193.0 60.9 reduce-scatter.4
  256.5 60.5 reduce-scatter.8
  319.5 60.6 reduce-scatter.6
  382.4 53.0 all-gather.10
  437.9 41.2 all-gather.8
  594.3 80.7 reduce-scatter.10
